TPU v7x, 32 devices: a whole 2x2x4 slice. The times are simulated.
32 devices in a mesh: grp: 2 (over x), seq: 4 (over y, core), tp: 4 (over z).
Axes of the slice: x: 2, y: 2, z: 4, core: 2. Of those that a mesh axis runs over, the one named last changes fastest.
Arguments:
- prompt: bfloat16 [2048, 5376], P(('grp', 'seq'), 'tp'), parts along dimension 0, may hold values from -8 to 8, as said below
- cont_ids: int32 [16, 64], P('grp'), parts along dimension 0, may hold values from 0 to 131071
- embed: bfloat16 [131072, 5376], P('seq', 'tp'), may hold values from -0.078125 to 0.078125
- pre_gain: float32 [5376], replicated, may hold values from 0.5 to 1.5
- w_query: bfloat16 [5376, 4096], P('seq', 'tp'), may hold values from -0.078125 to 0.078125
- w_keyval: bfloat16 [5376, 2, 2048], P('seq', None, 'tp'), may hold values from -0.078125 to 0.078125
- q_gain: float32 [128], replicated, may hold values from 0.25 to 1.75
- k_gain: float32 [128], replicated, may hold values from 0.25 to 1.75
- w_out: bfloat16 [4096, 5376], P('tp', 'seq'), may hold values from -0.09375 to 0.09375
- post_gain: float32 [5376], replicated, may hold values from 0.5 to 1.5
Outputs:
- prompt_out: bfloat16 [2048, 5376], P(('grp', 'seq'), 'tp'), parts along dimension 0
- cont_out: bfloat16 [16, 64, 5376], P(('grp', 'seq'), None, 'tp'), parts along dimension 0
There are 2 independent parts, one for each index of `grp`. A program takes and returns all parts, laid end to end along the dimension named above; an argument that names none is the same for every part. Nothing has to cross between parts.
Inputs may be any that keep to these rules, and one draw needn't show every extreme that they name: `prompt`: values are rough from entry to entry.
All inputs are finite; a program needn't handle non-finite values.
Results may differ from a plain program's by a relative error of at most 0.014.
Values may be sent and summed in bfloat16 or wider, within the bound.
No kernel may reach another device: no remote copies, remote signals or barrier semaphores. Data moves between devices by JAX's collectives and lax.ppermute only.
A program may use at most 256 MiB of HBM per device.

v0:
```python
import math
import jax
import jax.numpy as jnp
from jax import lax
from jax.sharding import PartitionSpec as P

WINDOW = 1024
eps_norm = 1e-06
query_scalar = 168.0
rope_base = 10000.0


def from_behind(value, axis, by):
    count = lax.axis_size(axis)
    pairs = [(i, i + by) for i in range(count) if 0 <= i + by < count]
    return lax.ppermute(value, axis, pairs)


def from_root(value, axis, root):
    mine = lax.axis_index(axis) == root
    return lax.psum(jnp.where(mine, value, jnp.zeros_like(value)), axis)


def rms_scale(values, gain):
    mean_sq = jnp.mean(values * values, axis=-1, keepdims=True)
    return values * lax.rsqrt(mean_sq + eps_norm) * gain


def rotate(values, positions):
    half = values.shape[-1] // 2
    freqs = rope_base ** (
        -(jnp.arange(half, dtype=jnp.int32).astype(jnp.float32) * 2.0) / values.shape[-1]
    )
    angles = positions.astype(jnp.float32)[:, None] * freqs[None, :]
    cosine = jnp.cos(angles)[:, None, :]
    sine = jnp.sin(angles)[:, None, :]
    first = values[..., :half]
    second = values[..., half:]
    return jnp.concatenate(
        [first * cosine - second * sine, second * cosine + first * sine], axis=-1
    )


def attend(queries, keys, values, allowed):
    rows, heads, width = queries.shape
    kv_heads = keys.shape[1]
    grouped = queries.reshape(rows, kv_heads, heads // kv_heads, width)
    scores = jnp.einsum(
        "qkgd,nkd->kgqn", grouped, keys, preferred_element_type=jnp.float32
    ) * query_scalar ** (-0.5)
    scores = jnp.where(allowed[None, None], scores, -1e30)
    top = jnp.max(scores, axis=-1, keepdims=True)
    weights = jnp.exp(scores - top)
    weights = (weights / jnp.sum(weights, axis=-1, keepdims=True)).astype(jnp.bfloat16)
    mixed = jnp.einsum("kgqn,nkd->qkgd", weights, values, preferred_element_type=jnp.float32)
    return mixed.reshape(rows, heads * width).astype(jnp.bfloat16)


def on_device(
    prompt, cont_ids, embed, pre_gain, w_query, w_keyval, q_gain, k_gain, w_out, post_gain
):
    tok_rows, local_cols = prompt.shape
    n_seq = lax.axis_size("seq")
    n_tp = lax.axis_size("tp")
    seq_index = lax.axis_index("seq")
    tp_index = lax.axis_index("tp")
    full_width = local_cols * n_tp
    cont_count, cont_len = cont_ids.shape
    own_conts = cont_count // n_seq
    cont_rows = own_conts * cont_len
    vocab_rows = embed.shape[0]
    flat_ids = cont_ids.reshape(-1)
    vocab_start = seq_index * vocab_rows
    chosen = flat_ids - vocab_start
    inside = (chosen >= 0) & (chosen < vocab_rows)
    picked = jnp.take(embed, jnp.clip(chosen, 0, vocab_rows - 1), axis=0)
    embedded = lax.psum_scatter(
        jnp.where(inside[:, None], picked.astype(jnp.float32), 0.0).astype(jnp.bfloat16),
        "seq",
        scatter_dimension=0,
        tiled=True,
    ).astype(jnp.float32)
    cont_x = (embedded * math.sqrt(full_width)).astype(jnp.bfloat16)
    rows_x = jnp.concatenate([prompt, cont_x], axis=0)
    whole = lax.all_gather(rows_x, "tp", axis=1, tiled=True)
    normed = rms_scale(whole.astype(jnp.float32), pre_gain).astype(jnp.bfloat16)
    all_rows = normed.shape[0]
    q_cols = w_query.shape[1]
    kv_cols = w_keyval.shape[2]
    query_part = jnp.dot(
        normed,
        lax.all_gather(w_query, "seq", axis=0, tiled=True),
        preferred_element_type=jnp.float32,
    )
    kv_part = jnp.einsum(
        "rd,dcf->rcf",
        normed,
        lax.all_gather(w_keyval, "seq", axis=0, tiled=True),
        preferred_element_type=jnp.float32,
    )
    head_dim = q_gain.shape[0]
    q_heads = q_cols // head_dim
    kv_heads = kv_cols // head_dim
    tokens_total = n_seq * tok_rows
    positions = jnp.concatenate(
        [
            seq_index * tok_rows + jnp.arange(tok_rows, dtype=jnp.int32),
            tokens_total + jnp.arange(cont_rows, dtype=jnp.int32) % cont_len,
        ]
    )
    queries = rotate(
        rms_scale(query_part.reshape(all_rows, q_heads, head_dim), q_gain), positions
    ).astype(jnp.bfloat16)
    keys = rotate(
        rms_scale(kv_part[:, 0].reshape(all_rows, kv_heads, head_dim), k_gain), positions
    ).astype(jnp.bfloat16)
    values = kv_part[:, 1].astype(jnp.bfloat16)
    keyval = jnp.stack([keys.reshape(all_rows, kv_cols), values], axis=1)
    prompt_kv = keyval[:tok_rows]
    cont_kv = keyval[tok_rows:]
    reach = WINDOW // tok_rows
    earlier = []
    moving = prompt_kv
    for step in range(reach):
        moving = from_behind(moving, "seq", 1)
        earlier = [moving] + earlier
    band = jnp.concatenate(earlier + [prompt_kv], axis=0)
    q_pos = positions[:tok_rows]
    key_pos = seq_index * tok_rows - reach * tok_rows + jnp.arange(band.shape[0], dtype=jnp.int32)
    allowed = (
        (key_pos[None, :] <= q_pos[:, None])
        & (key_pos[None, :] > q_pos[:, None] - WINDOW)
        & (key_pos[None, :] >= 0)
    )
    prompt_mix = attend(
        queries[:tok_rows],
        band[:, 0].reshape(-1, kv_heads, head_dim),
        band[:, 1].reshape(-1, kv_heads, head_dim),
        allowed,
    )
    final = from_root(band[band.shape[0] - WINDOW :], "seq", n_seq - 1)
    spots = jnp.arange(cont_len, dtype=jnp.int32)
    allowed_cont = jnp.concatenate(
        [
            jnp.arange(WINDOW, dtype=jnp.int32)[None, :] > spots[:, None],
            spots[None, :] <= spots[:, None],
        ],
        axis=1,
    )
    cont_q = queries[tok_rows:].reshape(own_conts, cont_len, q_heads, head_dim)
    cont_keys = cont_kv.reshape(own_conts, cont_len, 2, kv_cols)

    def one_cont(query_block, key_block):
        joined = jnp.concatenate([final, key_block], axis=0)
        return attend(
            query_block,
            joined[:, 0].reshape(-1, kv_heads, head_dim),
            joined[:, 1].reshape(-1, kv_heads, head_dim),
            allowed_cont,
        )

    cont_mix = jax.vmap(one_cont)(cont_q, cont_keys).reshape(cont_rows, q_cols)
    mixed = jnp.concatenate([prompt_mix, cont_mix], axis=0)
    partial_rows = jnp.dot(
        mixed, lax.all_gather(w_out, "seq", axis=1, tiled=True), preferred_element_type=jnp.float32
    )
    attn_proj = lax.psum_scatter(
        partial_rows.astype(jnp.bfloat16), "tp", scatter_dimension=1, tiled=True
    ).astype(jnp.float32)
    row_sq = lax.psum(jnp.sum(attn_proj * attn_proj, axis=1), "tp")
    factor = lax.rsqrt(row_sq / full_width + eps_norm)
    gain_part = lax.dynamic_slice_in_dim(post_gain, tp_index * local_cols, local_cols)
    result = (rows_x.astype(jnp.float32) + attn_proj * factor[:, None] * gain_part).astype(
        jnp.bfloat16
    )
    return (result[:tok_rows], result[tok_rows:].reshape(own_conts, cont_len, local_cols))


def solution(mesh):
    return jax.shard_map(
        on_device,
        mesh=mesh,
        in_specs=(
            P(("grp", "seq"), "tp"),
            P("grp", None),
            P("seq", "tp"),
            P(),
            P("seq", "tp"),
            P("seq", None, "tp"),
            P(),
            P(),
            P("tp", "seq"),
            P(),
        ),
        out_specs=(P(("grp", "seq"), "tp"), P(("grp", "seq"), None, "tp")),
        check_vma=False,
    )
```

profile of v0, /device:TPU:0, one launch (start us, length us, event | category | flops | bytes accessed | tf_op | source)
XLA Modules:
  0.0 655.2 jit_solution(15897168828762125381)
XLA Ops:
  7.2 0.7 subtract_clamp_fusion
  8.1 0.7 compare_and_fusion
  8.8 106.7 %copy.74 = bf16[32768,1344]{1,0:T(8,128)(2,1)} copy(bf16[32768,1344]{0,1:T(8,128)(2,1)} %param.12) | data formatting | bytes 176160768 | tf_op args[2]
  115.5 15.7 %gather_fusion = bf16[512,1344]{1,0:T(8,128)(2,1)S(1)} fusion(bf16[32768,1344]{1,0:T(8,128)(2,1)} %copy.74, s32[1024]{0:T(1024)S(1)} %pad_clamp_fusion), kind=kCustom, calls=%fused_computation | custom fusion | bytes 2754560 | tf_op jit(solution)/shard_map/jit(_take)/gather | solution.py:76
  131.2 0.7 copy.75
  132.3 1.5 copy.108
  133.9 31.7 %reduce-scatter.7.cloned.1.call-done = bf16[128,1344]{1,0:T(8,128)(2,1)} async-done(((bf16[512,1344]{1,0:T(8,128)(2,1)}), bf16[128,1344]{1,0:T(8,128)(2,1)}) %reduce-scatter.7.cloned.1.call-update) | async-done | bytes 344080
  165.6 1.2 copy.109
  166.9 2.2 pad_maximum_fusion.1
  169.2 1.9 copy.76
  171.2 0.5 all-gather.9.cloned.1.call-update
  172.2 0.8 multiply_cosine_fusion
  172.9 76.0 %all-gather.5.cloned.1.call-done = bf16[384,5376]{0,1:T(8,128)(2,1)} async-done(((bf16[384,1344]{0,1:T(8,128)(2,1)}), bf16[384,5376]{0,1:T(8,128)(2,1)}) %all-gather.5.cloned.1.call-update) | async-done | bytes 4128784 | tf_op jit(solution)/shard_map/all_gather | solution.py:85
  249.0 3.1 fusion.3
  252.1 70.1 %all-gather.7.cloned.1.call-done = bf16[5376,2,512]{2,0,1:T(8,128)(2,1)} async-done(((bf16[1344,2,512]{2,0,1:T(8,128)(2,1)}), bf16[5376,2,512]{2,0,1:T(8,128)(2,1)}) %all-gather.7.cloned.1.call-update) | async-done | bytes 11010064 | tf_op jit(solution)/shard_map/all_gather | solution.py:98
  322.2 9.9 %fusion.12 = f32[384,2,512]{2,0,1:T(8,128)S(1)} fusion(bf16[5376,2,512]{2,0,1:T(8,128)(2,1)} %all-gather.7.cloned.1.call-done, bf16[384,5376]{0,1:T(8,128)(2,1)} %all-gather.5.cloned.1.call-done, f32[5376]{0:T(1024)S(1)} %copy-done.16, f32[384]{0:T(512)S(1)} %add_rsqrt_fusion.3), kind=kOutput, calls=%fused_computation.25 | convolution fusion | flops 4236115968 | bytes 16734720 | tf_op jit(solution)/shard_map/rd,dcf->rcf/dot_general | solution.py:95
  332.5 0.5 multiply_reduce_fusion.1
  333.1 0.5 multiply_multiply_fusion
  333.6 0.7 subtract_convert_fusion.1
  334.2 0.5 pad_maximum_fusion.2
  335.0 2.2 collective-permute-start
  337.2 2.2 collective-permute-done
  339.5 17.3 %collective-permute-start.1 = (bf16[256,2,512]{2,0,1:T(8,128)(2,1)S(1)}, bf16[256,2,512]{2,0,1:T(8,128)(2,1)S(1)}, u32[]{:S(2)}, u32[]{:S(2)}) collective-permute-start(bf16[256,2,512]{2,0,1:T(8,128)(2,1)S(1)} %collective-permute-done), channel_id=1, source_target_pairs={{0,4},{4,8},{8,12},{1,5},{5,9},{9,13},{2,6},{6,10},{10,14},{3,7},{... | collective-permute-start | bytes 1572872 | tf_op jit(solution)/shard_map/ppermute | solution.py:16
  356.8 1.5 collective-permute-done.1
  358.3 20.4 %collective-permute-start.2 = (bf16[256,2,512]{2,0,1:T(8,128)(2,1)S(1)}, bf16[256,2,512]{2,0,1:T(8,128)(2,1)S(1)}, u32[]{:S(2)}, u32[]{:S(2)}) collective-permute-start(bf16[256,2,512]{2,0,1:T(8,128)(2,1)S(1)} %collective-permute-done.1), channel_id=1, source_target_pairs={{0,4},{4,8},{8,12},{1,5},{5,9},{9,13},{2,6},{6,10},{10,14},{3,7},{... | collective-permute-start | bytes 1572872 | tf_op jit(solution)/shard_map/ppermute | solution.py:16
  378.6 1.5 collective-permute-done.2
  380.1 1.8 maximum_select_fusion
  382.0 0.5 all-gather.11.cloned.1.call-update
  382.5 0.6 reduce-scatter.5.cloned.1.call-start
  383.2 0.6 pad_add_fusion
  383.8 1.6 and_and_fusion
  385.4 24.4 %all-gather.9.cloned.1.call-done = bf16[5376,1024]{1,0:T(8,128)(2,1)} async-done(((bf16[1344,1024]{1,0:T(8,128)(2,1)}), bf16[5376,1024]{1,0:T(8,128)(2,1)}) %all-gather.9.cloned.1.call-update) | async-done | bytes 11010064 | tf_op jit(solution)/shard_map/all_gather | solution.py:92
  409.7 9.9 %fusion.27 = f32[384,1024]{1,0:T(8,128)S(1)} fusion(bf16[5376,1024]{1,0:T(8,128)(2,1)} %all-gather.9.cloned.1.call-done, bf16[384,5376]{0,1:T(8,128)(2,1)} %all-gather.5.cloned.1.call-done, f32[5376]{0:T(1024)S(1)} %copy-done.16, f32[384]{0:T(512)S(1)} %add_rsqrt_fusion.3), kind=kOutput, calls=%fused_computation.50 | convolution fusion | flops 4236115968 | bytes 16734720 | tf_op jit(solution)/shard_map/dot_general | solution.py:90
  420.0 1.2 multiply_reduce_fusion
  421.2 1.0 copy.80
  422.2 0.8 pad_maximum_fusion.4
  422.9 2.0 copy.86
  424.9 0.5 fusion.22
  425.4 0.5 copy-done.5
  425.9 2.1 collective-permute-start.3
  428.0 0.6 subtract_convert_fusion
  428.6 0.9 pad_maximum_fusion.3
  429.5 1.1 fusion.38
  431.0 1.3 reshape_squeeze.11
  432.3 1.4 copy.100
  433.8 4.8 fusion.65
  438.6 6.8 %fusion.25 = bf16[4,128,2,256]{3,1,2,0:T(8,128)(2,1)} fusion(bf16[1280,4,128,1]{0,2,3,1:T(8,128)(2,1)S(1)} %bitcast.77, f32[4,2,256]{2,1,0:T(2,128)S(1)} %fusion.65, pred[256,1280]{0,1:T(8,128)(4,1)} %and_and_fusion, bf16[256,4,2,128]{3,0,2,1:T(8,128)(2,1)S(1)} %bitcast.80, bf16[1280,4,128,1]{2,1,0,3:T(4,128)(2,1)S(1)} %bitcast.76), kind=kOutput, calls=%fused_computation.48 | convolution fusion | flops 1355549952 | bytes 4005888 | tf_op jit(solution)/shard_map/kgqn,nkd->qkgd/dot_general | solution.py:55
  445.4 24.7 %all-reduce.2.cloned.1.call-done = bf16[1024,2,512]{2,0,1:T(8,128)(2,1)} async-done(((bf16[1024,2,512]{2,0,1:T(8,128)(2,1)}), bf16[1024,2,512]{2,0,1:T(8,128)(2,1)}) %all-reduce.2.cloned.1.call-update) | async-done | bytes 2097168 | tf_op jit(solution)/shard_map/psum | solution.py:21
  470.0 3.0 copy.85
  473.1 0.5 broadcast_in_dim.53
  473.6 0.5 copy-done.6
  474.1 1.8 pad_maximum_fusion
  475.9 6.0 exponential_reduce_fusion
  482.0 4.4 fusion.30
  486.3 0.4 copy.107
  487.0 57.7 %all-gather.11.cloned.1.call-done = bf16[1024,5376]{0,1:T(8,128)(2,1)} async-done(((bf16[1024,1344]{0,1:T(8,128)(2,1)}), bf16[1024,5376]{0,1:T(8,128)(2,1)}) %all-gather.11.cloned.1.call-update) | async-done | bytes 11010064 | tf_op jit(solution)/shard_map/all_gather | solution.py:165
  544.7 11.5 %convolution_convert_fusion = bf16[384,5376]{0,1:T(8,128)(2,1)} fusion(bf16[1024,5376]{0,1:T(8,128)(2,1)} %all-gather.11.cloned.1.call-done, bf16[128,1024]{0,1:T(8,128)(2,1)S(1)} %reshape.287, bf16[256,1024]{0,1:T(8,128)(2,1)S(1)} %bitcast.84), kind=kOutput, calls=%fused_computation.9 | convolution fusion | flops 4231495680 | bytes 15925248 | tf_op jit(solution)/shard_map/dot_general | solution.py:164
  556.3 0.8 dynamic_slice.3
  557.1 75.0 %reduce-scatter.5.cloned.1.call-done = bf16[384,1344]{0,1:T(8,128)(2,1)} async-done(((bf16[384,5376]{0,1:T(8,128)(2,1)}), bf16[384,1344]{0,1:T(8,128)(2,1)}) %reduce-scatter.5.cloned.1.call-update) | async-done | bytes 1032208 | tf_op jit(solution)/shard_map/reduce_scatter | solution.py:167
  632.2 1.5 fusion.18
  633.7 11.0 %psum.15 = f32[384]{0:T(512)S(1)} all-reduce(f32[384]{0:T(512)S(1)} %fusion.18), channel_id=1, replica_groups=mesh['grp'=2,'seq'=4,'tp'=4] {'tp'}, use_global_device_ids=true, to_apply=%region_11.12 | all-reduce | flops 384 | bytes 3072 | tf_op jit(solution)/shard_map/psum | solution.py:170
  644.6 1.6 fusion.21
  646.3 0.9 slice.83
  647.2 0.9 copy.92
  (81 shorter events, 3.1 us)
Async XLA Ops:
  7.2 158.5 %reduce-scatter.7.cloned.1.call-start = ((), (), s32[]{:S(2)}) async-start(), calls=%async_computation.8 | async-start | bytes 1802240
  133.8 35.4 %copy-start = (bf16[1344,2,512]{2,1,0:T(2,128)(2,1)S(1)}, bf16[1344,2,512]{2,1,0:T(2,128)(2,1)}, u32[]{:S(2)}) copy-start(bf16[1344,2,512]{2,1,0:T(2,128)(2,1)} %param.15) | copy-start | bytes 8257540
  133.9 115.1 %all-gather.5.cloned.1.call-start = ((), (), s32[]{:S(2)}) async-start(), calls=%async_computation.2 | async-start | bytes 5160960 | tf_op jit(solution)/shard_map/all_gather | solution.py:85
  169.2 153.1 %all-gather.7.cloned.1.call-start = ((), (), s32[]{:S(2)}) async-start(), calls=%async_computation.3 | async-start | bytes 13762560 | tf_op jit(solution)/shard_map/all_gather | solution.py:98
  171.2 238.6 %all-gather.9.cloned.1.call-start = ((), (), s32[]{:S(2)}) async-start(), calls=%async_computation.4 | async-start | bytes 13762560 | tf_op jit(solution)/shard_map/all_gather | solution.py:92
  171.8 150.4 %copy-start.16 = (f32[5376]{0:T(1024)S(1)}, f32[5376]{0:T(1024)}, u32[]{:S(2)}) copy-start(f32[5376]{0:T(1024)} %param.13) | copy-start | bytes 64516
  171.8 298.3 %all-reduce.2.cloned.1.call-start = ((), (), s32[]{:S(2)}) async-start(), calls=%async_computation.5 | async-start | bytes 4194304 | tf_op jit(solution)/shard_map/psum | solution.py:21
  172.9 160.6 %copy-start.7 = (f32[384,64]{1,0:T(8,128)}, f32[384,64]{1,0:T(8,128)S(1)}, u32[]{:S(2)}) copy-start(f32[384,64]{1,0:T(8,128)S(1)} %get-tuple-element.13) | copy-start | bytes 294916
  332.1 0.9 copy-start.14
  335.0 4.4 collective-permute-start
  339.5 18.8 %collective-permute-start.1 = (bf16[256,2,512]{2,0,1:T(8,128)(2,1)S(1)}, bf16[256,2,512]{2,0,1:T(8,128)(2,1)S(1)}, u32[]{:S(2)}, u32[]{:S(2)}) collective-permute-start(bf16[256,2,512]{2,0,1:T(8,128)(2,1)S(1)} %collective-permute-done), channel_id=1, source_target_pairs={{0,4},{4,8},{8,12},{1,5},{5,9},{9,13},{2,6},{6,10},{10,14},{3,7},{... | collective-permute-start | bytes 1572872 | tf_op jit(solution)/shard_map/ppermute | solution.py:16
  358.3 23.7 %copy-start.2 = (bf16[256,2,512]{2,0,1:T(8,128)(2,1)}, bf16[256,2,512]{2,0,1:T(8,128)(2,1)S(1)}, u32[]{:S(2)}) copy-start(bf16[256,2,512]{2,0,1:T(8,128)(2,1)S(1)} %collective-permute-done.1) | copy-start | bytes 1572868
  358.3 21.8 %collective-permute-start.2 = (bf16[256,2,512]{2,0,1:T(8,128)(2,1)S(1)}, bf16[256,2,512]{2,0,1:T(8,128)(2,1)S(1)}, u32[]{:S(2)}, u32[]{:S(2)}) collective-permute-start(bf16[256,2,512]{2,0,1:T(8,128)(2,1)S(1)} %collective-permute-done.1), channel_id=1, source_target_pairs={{0,4},{4,8},{8,12},{1,5},{5,9},{9,13},{2,6},{6,10},{10,14},{3,7},{... | collective-permute-start | bytes 1572872 | tf_op jit(solution)/shard_map/ppermute | solution.py:16
  380.1 1.8 copy-start.4
  381.9 162.8 %all-gather.11.cloned.1.call-start = ((), (), s32[]{:S(2)}) async-start(), calls=%async_computation.6 | async-start | bytes 13762560 | tf_op jit(solution)/shard_map/all_gather | solution.py:165
  382.5 249.6 %reduce-scatter.5.cloned.1.call-start = ((), (), s32[]{:S(2)}) async-start(), calls=%async_computation.7 | async-start | bytes 5160960 | tf_op jit(solution)/shard_map/reduce_scatter | solution.py:167
  420.0 4.9 copy-start.15
  424.9 1.0 copy-start.5
  424.9 3.1 copy-start.8
  425.9 4.7 collective-permute-start.3
  428.6 2.1 copy-start.3
  431.0 2.8 copy-start.11
  432.3 1.5 copy-start.9
  433.8 4.8 copy-start.10
  473.0 1.0 copy-start.6
  474.1 1.8 copy-start.12
  474.1 1.8 copy-start.13
  482.0 62.8 %copy-start.17 = (bf16[4,128,2,256]{3,1,2,0:T(8,128)(2,1)S(1)}, bf16[4,128,2,256]{3,1,2,0:T(8,128)(2,1)}, u32[]{:S(2)}) copy-start(bf16[4,128,2,256]{3,1,2,0:T(8,128)(2,1)} %fusion.25) | copy-start | bytes 1572868
  556.2 88.4 %copy-start.1 = (bf16[256,1344]{0,1:T(8,128)(2,1)S(1)}, bf16[256,1344]{0,1:T(8,128)(2,1)}, u32[]{:S(2)}) copy-start(bf16[256,1344]{0,1:T(8,128)(2,1)} %param.10) | copy-start | bytes 2064388
Sparse Core Ops, SparseCore 0:
  134.0 31.5 reduce-scatter.6
  169.3 79.6 all-gather.4
  250.5 71.6 all-gather.6
  323.6 86.0 all-gather.8
  412.0 58.0 all-reduce.1
  471.5 73.2 all-gather.10
  556.4 75.7 reduce-scatter.4
where the time goes:
time: 663 us; the launch traced here: 655 us
  waiting for transfers between devices  366 us (55%)
  local copies, waits for them, and re-layouts  143 us (22%)
  matrix products  53.3 us (8%)
  starting transfers between devices  43 us (6%)
  other arithmetic  24.2 us (4%)
  between operations  14.9 us (2%)
  blocking collectives  11 us (2%)
    unnamed x45, local copies, waits for them, and re-layouts  113 us
    all_gather x1, waiting for transfers between devices, on_device(): whole = lax.all_gather(rows_x, 'tp', axis=1, tiled=True)  76 us
    reduce_scatter x1, waiting for transfers between devices, on_device(): lax.psum_scatter(partial_rows.astype(jnp.bfloat16), 'tp', scatter_dimensi...  75 us
    all_gather x1, waiting for transfers between devices, on_device(): lax.all_gather(w_keyval, 'seq', axis=0, tiled=True)  70.1 us
    all_gather x1, waiting for transfers between devices, on_device(): lax.all_gather(w_out, 'seq', axis=1, tiled=True)  57.7 us
    ppermute x4, starting transfers between devices, from_behind(): return lax.ppermute(value, axis, pairs)  41.9 us
    unnamed x8, waiting for transfers between devices  32.8 us
    psum x1, waiting for transfers between devices, from_root(): return lax.psum(jnp.where(mine, value, jnp.zeros_like(value)), axis)  24.7 us
  transfers between devices with their start and end apart: 11, of which 10 were waited for; matrix products, arithmetic and copies ran while one was open for 11% of the time, Pallas kernels for 0%

commit v1 on v0

--- a/solution.py
+++ b/solution.py
@@ -8,6 +8,16 @@
 eps_norm = 1e-06
 query_scalar = 168.0
 rope_base = 10000.0
+
+
+def gather_by_hops(x, mesh_axis, along):
+    size = lax.axis_size(mesh_axis)
+    block, pieces = (x, [x])
+    for _ in range(size - 1):
+        block = lax.ppermute(block, mesh_axis, [(i, (i + 1) % size) for i in range(size)])
+        pieces.insert(0, block)
+    line = jnp.concatenate(pieces, axis=along)
+    return jnp.roll(line, (lax.axis_index(mesh_axis) + 1) * x.shape[along], axis=along)
 
 
 def from_behind(value, axis, by):
@@ -82,7 +92,7 @@
     ).astype(jnp.float32)
     cont_x = (embedded * math.sqrt(full_width)).astype(jnp.bfloat16)
     rows_x = jnp.concatenate([prompt, cont_x], axis=0)
-    whole = lax.all_gather(rows_x, "tp", axis=1, tiled=True)
+    whole = gather_by_hops(rows_x, "tp", 1)
     normed = rms_scale(whole.astype(jnp.float32), pre_gain).astype(jnp.bfloat16)
     all_rows = normed.shape[0]
     q_cols = w_query.shape[1]

time: 663 us -> 576 us (0.87)
  waiting for transfers between devices: 366 us -> 247 us
  local copies, waits for them, and re-layouts: 143 us -> 159 us
  starting transfers between devices: 43 us -> 56.4 us
    all_gather x1 -> x0, waiting for transfers between devices: 76 us -> none  [on_device(): whole = lax.all_gather(rows_x, 'tp', axis=1, tiled=True)]
    ppermute x0 -> x3, waiting for transfers between devices: none -> 73.7 us  [gather_by_hops(): lax.ppermute(block, mesh_axis, [(i, (i + 1) % size) for i in range(size)])]
    all_gather x1, waiting for transfers between devices: 70.1 us -> 0.01 us  [on_device(): lax.all_gather(w_keyval, 'seq', axis=0, tiled=True)]
    all_gather x1, waiting for transfers between devices: 24.4 us -> 0.19 us  [on_device(): lax.all_gather(w_query, 'seq', axis=0, tiled=True)]
    psum x1, waiting for transfers between devices: 24.7 us -> 10.5 us  [from_root(): return lax.psum(jnp.where(mine, value, jnp.zeros_like(value)), axis)]
    ppermute x4, starting transfers between devices: 41.9 us -> 53.8 us  [from_behind(): return lax.ppermute(value, axis, pairs)]
    unnamed x45 -> x53, local copies, waits for them, and re-layouts: 113 us -> 124 us
    unnamed x8 -> x7, waiting for transfers between devices: 32.8 us -> 27.3 us
  transfers between devices with their start and end apart: 11 -> 13, of which waited for: 10 -> 11; matrix products, arithmetic and copies ran while one was open for 11% -> 17% of each run, Pallas kernels for 0% -> 0%
where the time goes in v1:
time: 576 us; the launch traced here: 568 us
  waiting for transfers between devices  247 us (43%)
  local copies, waits for them, and re-layouts  159 us (28%)
  starting transfers between devices  56.4 us (10%)
  matrix products  53.4 us (9%)
  other arithmetic  25.7 us (4%)
  between operations  14.9 us (3%)
  blocking collectives  11 us (2%)
    unnamed x53, local copies, waits for them, and re-layouts  124 us
    reduce_scatter x1, waiting for transfers between devices, on_device(): lax.psum_scatter(partial_rows.astype(jnp.bfloat16), 'tp', scatter_dimensi...  75.1 us
    ppermute x3, waiting for transfers between devices, gather_by_hops(): lax.ppermute(block, mesh_axis, [(i, (i + 1) % size) for i in range(size)])  73.7 us
    all_gather x1, waiting for transfers between devices, on_device(): lax.all_gather(w_out, 'seq', axis=1, tiled=True)  56.2 us
    ppermute x4, starting transfers between devices, from_behind(): return lax.ppermute(value, axis, pairs)  53.8 us
    unnamed x7, waiting for transfers between devices  27.3 us
    gather x2, local copies, waits for them, and re-layouts, on_device(): picked = jnp.take(embed, jnp.clip(chosen, 0, vocab_rows - 1), axis=0)  17.1 us
    dot_general x2, matrix products, attend(): jnp.einsum('kgqn,nkd->qkgd', weights, values, preferred_element_type=jnp....  12.1 us
  transfers between devices with their start and end apart: 13, of which 11 were waited for; matrix products, arithmetic and copies ran while one was open for 17% of the time, Pallas kernels for 0%

profile of v1, /device:TPU:0, one launch (start us, length us, event | category | flops | bytes accessed | tf_op | source)
XLA Modules:
  0.0 567.9 jit_solution(14346635820245175479)
XLA Ops:
  7.2 0.7 subtract_clamp_fusion
  8.1 0.7 compare_and_fusion
  8.8 106.8 %copy.74 = bf16[32768,1344]{1,0:T(8,128)(2,1)} copy(bf16[32768,1344]{0,1:T(8,128)(2,1)} %param.12) | data formatting | bytes 176160768 | tf_op args[2]
  115.6 16.5 %gather_fusion = bf16[512,1344]{1,0:T(8,128)(2,1)S(1)} fusion(bf16[32768,1344]{1,0:T(8,128)(2,1)} %copy.74, s32[1024]{0:T(1024)S(1)} %pad_clamp_fusion), kind=kCustom, calls=%fused_computation | custom fusion | bytes 2754560 | tf_op jit(solution)/shard_map/jit(_take)/gather | solution.py:86
  132.1 0.7 copy.75
  133.2 1.5 copy.108
  134.8 3.7 copy.76
  138.6 0.7 all-gather.6.cloned.1.call-update
  139.4 26.0 %reduce-scatter.7.cloned.1.call-done = bf16[128,1344]{1,0:T(8,128)(2,1)} async-done(((bf16[512,1344]{1,0:T(8,128)(2,1)}), bf16[128,1344]{1,0:T(8,128)(2,1)}) %reduce-scatter.7.cloned.1.call-update) | async-done | bytes 344080
  165.4 1.2 copy.109
  166.8 1.5 collective-permute-start
  168.3 24.7 %collective-permute-done = bf16[384,1344]{0,1:T(8,128)(2,1)S(1)} collective-permute-done((bf16[384,1344]{0,1:T(8,128)(2,1)S(1)}, bf16[384,1344]{0,1:T(8,128)(2,1)S(1)}, u32[]{:S(2)}, u32[]{:S(2)}) %collective-permute-start) | collective-permute-done | bytes 1032224 | tf_op jit(solution)/shard_map/ppermute | solution.py:17
  193.0 25.3 %collective-permute-done.1 = bf16[384,1344]{0,1:T(8,128)(2,1)S(1)} collective-permute-done((bf16[384,1344]{0,1:T(8,128)(2,1)S(1)}, bf16[384,1344]{0,1:T(8,128)(2,1)S(1)}, u32[]{:S(2)}, u32[]{:S(2)}) %collective-permute-start.1) | collective-permute-done | bytes 1032224 | tf_op jit(solution)/shard_map/ppermute | solution.py:17
  218.6 0.8 multiply_cosine_fusion
  219.4 23.7 %collective-permute-done.2 = bf16[384,1344]{0,1:T(8,128)(2,1)} collective-permute-done((bf16[384,1344]{0,1:T(8,128)(2,1)S(1)}, bf16[384,1344]{0,1:T(8,128)(2,1)}, u32[]{:S(2)}, u32[]{:S(2)}) %collective-permute-start.2) | collective-permute-done | bytes 1032224 | tf_op jit(solution)/shard_map/ppermute | solution.py:17
  243.1 2.3 constant_dynamic-update-slice_fusion.7
  245.4 1.1 constant_dynamic-update-slice_fusion.6
  246.5 1.1 constant_dynamic-update-slice_fusion.5
  247.6 1.1 constant_dynamic-update-slice_fusion.4
  248.8 2.4 constant_dynamic-update-slice_fusion.3
  251.2 1.1 constant_dynamic-update-slice_fusion.2
  252.3 1.1 constant_dynamic-update-slice_fusion.1
  253.4 1.1 constant_dynamic-update-slice_fusion
  254.5 3.9 fusion.3
  258.5 10.1 %fusion.12 = f32[384,2,512]{2,0,1:T(8,128)S(1)} fusion(bf16[5376,2,512]{2,0,1:T(8,128)(2,1)} %all-gather.4.cloned.1.call-done, f32[5376]{0:T(1024)S(1)} %copy-done.18, f32[384]{0:T(512)S(1)} %add_rsqrt_fusion.3, bf16[384,10752]{0,1:T(8,128)(2,1)} %constant_dynamic-update-slice_fusion, s32[]{:T(128)S(6)} %select_n.69), kind=kOutput, calls=%fused_computation.25 | convolution fusion | flops 4236115968 | bytes 16734724 | tf_op jit(solution)/shard_map/rd,dcf->rcf/dot_general | solution.py:105
  270.1 0.7 subtract_convert_fusion.1
  271.5 1.3 collective-permute-start.3
  272.9 1.5 collective-permute-done.3
  274.3 20.0 %collective-permute-start.4 = (bf16[256,2,512]{2,0,1:T(8,128)(2,1)S(1)}, bf16[256,2,512]{2,0,1:T(8,128)(2,1)S(1)}, u32[]{:S(2)}, u32[]{:S(2)}) collective-permute-start(bf16[256,2,512]{2,0,1:T(8,128)(2,1)S(1)} %collective-permute-done.3), channel_id=1, source_target_pairs={{0,4},{4,8},{8,12},{1,5},{5,9},{9,13},{2,6},{6,10},{10,14},{3,7},{... | collective-permute-start | bytes 1572872 | tf_op jit(solution)/shard_map/ppermute | solution.py:26
  294.3 1.5 collective-permute-done.4
  295.8 20.4 %collective-permute-start.5 = (bf16[256,2,512]{2,0,1:T(8,128)(2,1)S(1)}, bf16[256,2,512]{2,0,1:T(8,128)(2,1)S(1)}, u32[]{:S(2)}, u32[]{:S(2)}) collective-permute-start(bf16[256,2,512]{2,0,1:T(8,128)(2,1)S(1)} %collective-permute-done.4), channel_id=1, source_target_pairs={{0,4},{4,8},{8,12},{1,5},{5,9},{9,13},{2,6},{6,10},{10,14},{3,7},{... | collective-permute-start | bytes 1572872 | tf_op jit(solution)/shard_map/ppermute | solution.py:26
  316.2 1.5 collective-permute-done.5
  317.7 2.9 maximum_select_fusion
  321.2 0.6 reduce-scatter.5.cloned.1.call-start
  321.9 1.6 and_and_fusion
  323.7 10.0 %fusion.35 = f32[384,1024]{1,0:T(8,128)S(1)} fusion(bf16[5376,1024]{1,0:T(8,128)(2,1)} %all-gather.6.cloned.1.call-done, f32[5376]{0:T(1024)S(1)} %copy-done.18, f32[384]{0:T(512)S(1)} %add_rsqrt_fusion.3, bf16[384,10752]{0,1:T(8,128)(2,1)} %constant_dynamic-update-slice_fusion, s32[]{:T(128)S(6)} %select_n.69), kind=kOutput, calls=%fused_computation.64 | convolution fusion | flops 4236115968 | bytes 16734724 | tf_op jit(solution)/shard_map/dot_general | solution.py:100
  334.0 1.2 multiply_reduce_fusion
  335.2 1.0 copy.80
  336.2 0.8 pad_maximum_fusion.4
  336.9 2.0 copy.86
  339.9 12.2 %collective-permute-start.6 = (bf16[256,2,512]{2,0,1:T(8,128)(2,1)S(1)}, bf16[256,2,512]{2,0,1:T(8,128)(2,1)S(1)}, u32[]{:S(2)}, u32[]{:S(2)}) collective-permute-start(bf16[256,2,512]{2,0,1:T(8,128)(2,1)S(1)} %copy-done.6), channel_id=1, source_target_pairs={{0,4},{4,8},{8,12},{1,5},{5,9},{9,13},{2,6},{6,10},{10,14},{3,7},{... | collective-permute-start | bytes 1572872 | tf_op jit(solution)/shard_map/ppermute | solution.py:26
  352.1 0.6 subtract_convert_fusion
  352.8 0.9 pad_maximum_fusion.3
  353.6 1.1 fusion.38
  355.0 1.2 fusion.64
  356.2 3.8 reshape_squeeze.11
  360.1 1.4 copy.100
  361.5 5.1 fusion.67
  366.6 7.1 %fusion.25 = bf16[4,128,2,256]{3,1,2,0:T(8,128)(2,1)} fusion(bf16[1280,4,128,1]{0,2,3,1:T(8,128)(2,1)S(1)} %bitcast.77, f32[4,2,256]{2,1,0:T(2,128)S(1)} %fusion.67, pred[256,1280]{0,1:T(8,128)(4,1)S(1)} %copy-done.15, bf16[256,4,2,128]{3,0,2,1:T(8,128)(2,1)S(1)} %bitcast.80, bf16[1280,4,128,1]{2,1,0,3:T(4,128)(2,1)} %bitcast.76), kind=kOutput, calls=%fused_computation.48 | convolution fusion | flops 1355549952 | bytes 4005888 | tf_op jit(solution)/shard_map/kgqn,nkd->qkgd/dot_general | solution.py:65
  373.7 10.5 %all-reduce.2.cloned.1.call-done = bf16[1024,2,512]{2,0,1:T(8,128)(2,1)} async-done(((bf16[1024,2,512]{2,0,1:T(8,128)(2,1)}), bf16[1024,2,512]{2,0,1:T(8,128)(2,1)}) %all-reduce.2.cloned.1.call-update) | async-done | bytes 2097168 | tf_op jit(solution)/shard_map/psum | solution.py:31
  384.2 3.0 copy.85
  388.3 1.8 pad_maximum_fusion
  390.1 6.0 %exponential_reduce_fusion = (f32[2,4,2,64]{3,2,1,0:T(2,128)S(1)}, f32[2,4,2,64,1088]{4,3,2,1,0:T(8,128)}) fusion(pred[64,1088]{1,0:T(8,128)(4,1)S(1)} %pad_add_fusion, bf16[2,1088,4,128,1]{1,3,4,2,0:T(8,128)(2,1)} %bitcast.74, bf16[2,64,4,2,128]{4,1,0,3,2:T(8,128)(2,1)} %bitcast.82), kind=kOutput, calls=%fused_computation.24 | convolution fusion | flops 289670208 | bytes 7020544 | tf_op jit(solution)/shard_map/vmap()/sub | solution.py:63
  396.1 5.0 fusion.27
  401.1 1.3 copy.107
  402.7 56.2 %all-gather.8.cloned.1.call-done = bf16[1024,5376]{0,1:T(8,128)(2,1)} async-done(((bf16[1024,1344]{0,1:T(8,128)(2,1)}), bf16[1024,5376]{0,1:T(8,128)(2,1)}) %all-gather.8.cloned.1.call-update) | async-done | bytes 11010064 | tf_op jit(solution)/shard_map/all_gather | solution.py:175
  458.9 10.0 %convolution_convert_fusion = bf16[384,5376]{0,1:T(8,128)(2,1)} fusion(bf16[1024,5376]{0,1:T(8,128)(2,1)} %all-gather.8.cloned.1.call-done, bf16[128,1024]{0,1:T(8,128)(2,1)S(1)} %reshape.287, bf16[256,1024]{0,1:T(8,128)(2,1)} %bitcast.84), kind=kOutput, calls=%fused_computation.9 | convolution fusion | flops 4231495680 | bytes 15925248 | tf_op jit(solution)/shard_map/dot_general | solution.py:174
  469.0 0.8 dynamic_slice.8
  469.7 75.1 %reduce-scatter.5.cloned.1.call-done = bf16[384,1344]{0,1:T(8,128)(2,1)} async-done(((bf16[384,5376]{0,1:T(8,128)(2,1)}), bf16[384,1344]{0,1:T(8,128)(2,1)}) %reduce-scatter.5.cloned.1.call-update) | async-done | bytes 1032208 | tf_op jit(solution)/shard_map/reduce_scatter | solution.py:177
  544.8 1.5 fusion.18
  546.3 11.0 %psum.15 = f32[384]{0:T(512)S(1)} all-reduce(f32[384]{0:T(512)S(1)} %fusion.18), channel_id=1, replica_groups=mesh['grp'=2,'seq'=4,'tp'=4] {'tp'}, use_global_device_ids=true, to_apply=%region_11.12 | all-reduce | flops 384 | bytes 3072 | tf_op jit(solution)/shard_map/psum | solution.py:180
  557.3 1.6 fusion.21
  559.0 0.9 slice.83
  559.9 0.9 copy.92
  (94 shorter events, 7.2 us)
Async XLA Ops:
  7.2 158.2 %reduce-scatter.7.cloned.1.call-start = ((), (), s32[]{:S(2)}) async-start(), calls=%async_computation.7 | async-start | bytes 1802240
  134.8 123.7 %all-gather.4.cloned.1.call-start = ((), (), s32[]{:S(2)}) async-start(), calls=%async_computation.2 | async-start | bytes 13762560 | tf_op jit(solution)/shard_map/all_gather | solution.py:108
  138.6 28.1 %copy-start = (bf16[256,1344]{0,1:T(8,128)(2,1)S(1)}, bf16[256,1344]{0,1:T(8,128)(2,1)}, u32[]{:S(2)}) copy-start(bf16[256,1344]{0,1:T(8,128)(2,1)} %param.10) | copy-start | bytes 2064388
  138.6 185.1 %all-gather.6.cloned.1.call-start = ((), (), s32[]{:S(2)}) async-start(), calls=%async_computation.3 | async-start | bytes 13762560 | tf_op jit(solution)/shard_map/all_gather | solution.py:102
  139.3 244.9 %all-reduce.2.cloned.1.call-start = ((), (), s32[]{:S(2)}) async-start(), calls=%async_computation.4 | async-start | bytes 4194304 | tf_op jit(solution)/shard_map/psum | solution.py:31
  166.8 26.2 %collective-permute-start = (bf16[384,1344]{0,1:T(8,128)(2,1)S(1)}, bf16[384,1344]{0,1:T(8,128)(2,1)S(1)}, u32[]{:S(2)}, u32[]{:S(2)}) collective-permute-start(bf16[384,1344]{0,1:T(8,128)(2,1)S(1)} %pad_maximum_fusion.1), channel_id=1, source_target_pairs={{0,1},{1,2},{2,3},{3,0},{4,5},{5,6},{6,7},{7,4},{8,9},{9,10},{10,1... | collective-permute-start | bytes 3096584 | tf_op jit(solution)/shard_map/ppermute | solution.py:17
  193.0 25.3 %collective-permute-start.1 = (bf16[384,1344]{0,1:T(8,128)(2,1)S(1)}, bf16[384,1344]{0,1:T(8,128)(2,1)S(1)}, u32[]{:S(2)}, u32[]{:S(2)}) collective-permute-start(bf16[384,1344]{0,1:T(8,128)(2,1)S(1)} %collective-permute-done), channel_id=1, source_target_pairs={{0,1},{1,2},{2,3},{3,0},{4,5},{5,6},{6,7},{7,4},{8,9},{9,10},{10,1... | collective-permute-start | bytes 3096584 | tf_op jit(solution)/shard_map/ppermute | solution.py:17
  218.3 24.8 %collective-permute-start.2 = (bf16[384,1344]{0,1:T(8,128)(2,1)S(1)}, bf16[384,1344]{0,1:T(8,128)(2,1)}, u32[]{:S(2)}, u32[]{:S(2)}) collective-permute-start(bf16[384,1344]{0,1:T(8,128)(2,1)S(1)} %collective-permute-done.1), channel_id=1, source_target_pairs={{0,1},{1,2},{2,3},{3,0},{4,5},{5,6},{6,7},{7,4},{8,9},{9,10},{10,1... | collective-permute-start | bytes 3096584 | tf_op jit(solution)/shard_map/ppermute | solution.py:17
  219.4 50.6 %copy-start.9 = (f32[384,64]{1,0:T(8,128)}, f32[384,64]{1,0:T(8,128)S(1)}, u32[]{:S(2)}) copy-start(f32[384,64]{1,0:T(8,128)S(1)} %get-tuple-element.12) | copy-start | bytes 294916
  219.4 50.6 %copy-start.11 = (f32[384,64]{1,0:T(8,128)}, f32[384,64]{1,0:T(8,128)S(1)}, u32[]{:S(2)}) copy-start(f32[384,64]{1,0:T(8,128)S(1)} %get-tuple-element.13) | copy-start | bytes 294916
  253.4 5.1 copy-start.18
  268.6 0.9 copy-start.16
  271.5 1.3 copy-start.8
  271.5 2.8 collective-permute-start.3
  274.3 46.3 %copy-start.1 = (bf16[256,2,512]{2,0,1:T(8,128)(2,1)}, bf16[256,2,512]{2,0,1:T(8,128)(2,1)S(1)}, u32[]{:S(2)}) copy-start(bf16[256,2,512]{2,0,1:T(8,128)(2,1)S(1)} %collective-permute-done.3) | copy-start | bytes 1572868
  274.3 21.5 %collective-permute-start.4 = (bf16[256,2,512]{2,0,1:T(8,128)(2,1)S(1)}, bf16[256,2,512]{2,0,1:T(8,128)(2,1)S(1)}, u32[]{:S(2)}, u32[]{:S(2)}) collective-permute-start(bf16[256,2,512]{2,0,1:T(8,128)(2,1)S(1)} %collective-permute-done.3), channel_id=1, source_target_pairs={{0,4},{4,8},{8,12},{1,5},{5,9},{9,13},{2,6},{6,10},{10,14},{3,7},{... | collective-permute-start | bytes 1572872 | tf_op jit(solution)/shard_map/ppermute | solution.py:26
  295.8 24.8 %copy-start.3 = (bf16[256,2,512]{2,0,1:T(8,128)(2,1)}, bf16[256,2,512]{2,0,1:T(8,128)(2,1)S(1)}, u32[]{:S(2)}) copy-start(bf16[256,2,512]{2,0,1:T(8,128)(2,1)S(1)} %collective-permute-done.4) | copy-start | bytes 1572868
  295.8 21.8 %collective-permute-start.5 = (bf16[256,2,512]{2,0,1:T(8,128)(2,1)S(1)}, bf16[256,2,512]{2,0,1:T(8,128)(2,1)S(1)}, u32[]{:S(2)}, u32[]{:S(2)}) collective-permute-start(bf16[256,2,512]{2,0,1:T(8,128)(2,1)S(1)} %collective-permute-done.4), channel_id=1, source_target_pairs={{0,4},{4,8},{8,12},{1,5},{5,9},{9,13},{2,6},{6,10},{10,14},{3,7},{... | collective-permute-start | bytes 1572872 | tf_op jit(solution)/shard_map/ppermute | solution.py:26
  317.7 3.0 copy-start.5
  320.6 138.3 %all-gather.8.cloned.1.call-start = ((), (), s32[]{:S(2)}) async-start(), calls=%async_computation.5 | async-start | bytes 13762560 | tf_op jit(solution)/shard_map/all_gather | solution.py:175
  321.2 223.6 %reduce-scatter.5.cloned.1.call-start = ((), (), s32[]{:S(2)}) async-start(), calls=%async_computation.6 | async-start | bytes 5160960 | tf_op jit(solution)/shard_map/reduce_scatter | solution.py:177
  334.0 4.9 copy-start.17
  338.9 1.0 copy-start.6
  338.9 13.2 %copy-start.10 = (f32[384,64]{1,0:T(8,128)S(1)}, f32[384,64]{1,0:T(8,128)}, u32[]{:S(2)}) copy-start(f32[384,64]{1,0:T(8,128)} %copy-done.9) | copy-start | bytes 294916
  338.9 13.2 %copy-start.12 = (f32[384,64]{1,0:T(8,128)S(1)}, f32[384,64]{1,0:T(8,128)}, u32[]{:S(2)}) copy-start(f32[384,64]{1,0:T(8,128)} %copy-done.11) | copy-start | bytes 294916
  339.9 14.8 %collective-permute-start.6 = (bf16[256,2,512]{2,0,1:T(8,128)(2,1)S(1)}, bf16[256,2,512]{2,0,1:T(8,128)(2,1)S(1)}, u32[]{:S(2)}, u32[]{:S(2)}) collective-permute-start(bf16[256,2,512]{2,0,1:T(8,128)(2,1)S(1)} %copy-done.6), channel_id=1, source_target_pairs={{0,4},{4,8},{8,12},{1,5},{5,9},{9,13},{2,6},{6,10},{10,14},{3,7},{... | collective-permute-start | bytes 1572872 | tf_op jit(solution)/shard_map/ppermute | solution.py:26
  352.7 2.1 copy-start.4
  353.6 1.3 copy-start.2
  356.2 5.3 copy-start.14
  356.2 5.3 copy-start.15
  361.5 5.1 copy-start.13
  387.2 1.0 copy-start.7
Sparse Core Ops, SparseCore 0:
  134.9 30.4 reduce-scatter.6
  166.9 73.1 all-gather.3
  241.7 81.9 all-gather.5
  325.9 58.2 all-reduce.1
  385.6 73.2 all-gather.7
  469.1 75.6 reduce-scatter.4
